TPU v7x, 32 devices: a whole 2x2x4 slice. The times are simulated.
32 devices in a mesh: dp: 2 (over x), ts: 16 (over z, y, core).
Axes of the slice: x: 2, y: 2, z: 4, core: 2. Of those that a mesh axis runs over, the one named last changes fastest.
Arguments:
- clip_video: bfloat16 [64, 4, 40, 128], P(('dp', 'ts')), may hold values from -6 to 6
- conv_weight: bfloat16 [3, 3, 3, 128, 128], replicated, may hold values from -0.109375 to 0.109375
- embed_weight: bfloat16 [128, 5120], replicated, may hold values from -0.5 to 0.5
- gain_spatial: float32 [5120], replicated, may hold values from 0.5 to 1.5
- gain_temporal: float32 [5120], replicated, may hold values from 0.5 to 1.5
- input_spatial: bfloat16 [5120, 384], P(('dp', 'ts')), may hold values from -0.078125 to 0.078125
- input_temporal: bfloat16 [5120, 384], P(('dp', 'ts')), may hold values from -0.078125 to 0.078125
- output_spatial: bfloat16 [128, 5120], replicated, may hold values from -2 to 2
- output_temporal: bfloat16 [128, 5120], replicated, may hold values from -2 to 2
- cotangent: bfloat16 [64, 4, 40, 5120], P(('dp', 'ts')), may hold values from -6 to 6
Outputs:
- layer_output: bfloat16 [64, 4, 40, 5120], P(('dp', 'ts'))
- grad_spatial: float32 [5120, 384], P(('dp', 'ts'))
All inputs are finite; a program needn't handle non-finite values.
Results may differ from a plain program's by a relative error of at most 0.015.
Values may be sent and summed in bfloat16 or wider, within the bound.
A program may use at most 128 MiB of HBM per device.

v0:
```python
import jax
import jax.numpy as jnp
from jax import lax
from jax.sharding import PartitionSpec as P

FR = 16
epsilon = 1e-06
masked = -1e30
F32 = jnp.float32
BF16 = jnp.bfloat16


def mm(a, b, dims=((1,), (0,))):
    return lax.dot_general(a, b, (dims, ((), ())), preferred_element_type=F32)


def mm_t(a, b):
    return mm(a, b, ((1,), (1,)))


def t_mm(a, b):
    return mm(a, b, ((0,), (0,)))


def wide_mm(a, b):
    high = b.astype(BF16)
    low = (b - high.astype(F32)).astype(BF16)
    return mm(a, high) + mm(a, low)


def conv_local(volume, weight, count):
    frames, height, columns, channels = volume.shape
    padded = jnp.pad(volume, ((0, 0), (1, 1), (1, 1), (0, 0)))
    summed = jnp.zeros((count * height * columns, weight.shape[-1]), F32)
    for a in range(3):
        for b in range(3):
            for e in range(3):
                window = padded[2 - a : 2 - a + count, b : b + height, e : e + columns, :]
                summed = summed + mm(window.reshape(-1, channels), weight[a, b, e])
    return summed


def attend_forward(q, k, v, allowed):
    scores = mm_t(q, k) * q.shape[-1] ** (-0.5)
    scores = jnp.where(allowed, scores, masked)
    raised = jnp.exp(scores - jnp.max(scores, axis=-1, keepdims=True))
    attend = raised / jnp.sum(raised, axis=-1, keepdims=True)
    return (mm(attend.astype(BF16), v).astype(BF16), attend)


def attend_backward(q, k, v, attend, g):
    scale = q.shape[-1] ** (-0.5)
    grad_attend = mm_t(g, v)
    grad_values = t_mm(attend.astype(BF16), g)
    inner = jnp.sum(grad_attend * attend, axis=-1, keepdims=True)
    grad_scores = (attend * (grad_attend - inner)).astype(BF16)
    grad_q = mm(grad_scores, k) * scale
    grad_k = t_mm(grad_scores, q) * scale
    return jnp.concatenate([grad_q, grad_k, grad_values], axis=-1).astype(BF16)


def shards(
    clip_video,
    conv_weight,
    embed_weight,
    gain_spatial,
    gain_temporal,
    input_spatial,
    input_temporal,
    output_spatial,
    output_temporal,
    cotangent,
):
    frames, height, columns, channels = clip_video.shape
    rows, triple = input_spatial.shape
    head = triple // 3
    width = embed_weight.shape[-1]
    places = height * columns
    tokens = frames * places
    ts = lax.axis_size("ts")
    team = FR // frames
    share = places // team
    groups = [[c * team + i for i in range(team)] for c in range(ts // team)]
    me = lax.axis_index("dp") * ts + lax.axis_index("ts")
    route = [(i - 1, i) for i in range(1, ts)]
    prior = lax.ppermute(clip_video, "ts", route)
    volume = jnp.concatenate([prior, clip_video], axis=0)
    basis = jnp.concatenate([embed_weight, output_spatial], axis=0)
    window = lax.dynamic_slice(basis, (0, me * rows), (basis.shape[0], rows)).astype(F32)
    gain_s = lax.dynamic_slice(gain_spatial, (me * rows,), (rows,))
    gain_t = lax.dynamic_slice(gain_temporal, (me * rows,), (rows,))
    embed_rows = (window[:channels] * gain_s).astype(BF16)
    part = jnp.concatenate(
        [mm(embed_rows, input_spatial), mm((window * gain_t).astype(BF16), input_temporal)], axis=0
    )
    mixed = lax.psum(part.astype(BF16), ("dp", "ts"))
    map_space, map_time = (mixed[:channels], mixed[channels:])
    gram = mm_t(basis, basis)
    cotangent_rows = cotangent.reshape(tokens, width)
    grad_mix_time = mm_t(cotangent_rows, output_temporal).astype(BF16)
    grad_direct = mm_t(cotangent_rows, output_spatial)
    features = jax.nn.gelu(conv_local(volume, conv_weight, frames), approximate=True).astype(BF16)
    squares = jnp.sum(
        wide_mm(features, gram[:channels, :channels]) * features.astype(F32), axis=-1, keepdims=True
    )
    factor_one = lax.rsqrt(jnp.maximum(squares, 0.0) / width + epsilon)
    packed_one = (mm(features, map_space) * factor_one).astype(BF16)
    place = jnp.arange(tokens)
    same_frame = place[:, None] // places == place[None, :] // places
    q, k, v = (packed_one[:, :head], packed_one[:, head : 2 * head], packed_one[:, 2 * head :])
    mixture_one, attend_one = attend_forward(q, k, v, same_frame)
    joint = jnp.concatenate([features, mixture_one], axis=-1)
    spread = wide_mm(joint, gram)
    squares = jnp.sum(spread * joint.astype(F32), axis=-1, keepdims=True)
    factor_two = lax.rsqrt(jnp.maximum(squares, 0.0) / width + epsilon)
    packed_two = (mm(joint, map_time) * factor_two).astype(BF16)
    sent = jnp.concatenate([packed_two, grad_mix_time], axis=-1).reshape(frames, places, 4 * head)
    got = lax.all_to_all(
        sent, "ts", split_axis=1, concat_axis=0, tiled=True, axis_index_groups=groups
    ).reshape(FR * share, 4 * head)
    spot = jnp.arange(FR * share)
    allowed = (spot[:, None] % share == spot[None, :] % share) & (spot[:, None] >= spot[None, :])
    tq, tk, tv, tg = (got[:, i * head : (i + 1) * head] for i in range(4))
    mixture_two, attend_two = attend_forward(tq, tk, tv, allowed)
    grad_two = attend_backward(tq, tk, tv, attend_two, tg)
    back = jnp.concatenate([mixture_two, grad_two], axis=-1).reshape(FR, share, 4 * head)
    home = lax.all_to_all(
        back, "ts", split_axis=0, concat_axis=1, tiled=True, axis_index_groups=groups
    ).reshape(tokens, 4 * head)
    mixture_two, grad_two = (home[:, :head], home[:, head:])
    output = mm(
        jnp.concatenate([joint, mixture_two], axis=-1),
        jnp.concatenate([basis, output_temporal], axis=0),
    ).astype(BF16)
    inner = jnp.sum(grad_two.astype(F32) * packed_two.astype(F32), axis=-1, keepdims=True)
    grad_mix_one = (
        grad_direct
        + factor_two * mm_t(grad_two, map_time[channels:])
        - factor_two**2 * inner / width * spread[:, channels:]
    ).astype(BF16)
    grad_one = attend_backward(q, k, v, attend_one, grad_mix_one)
    scaled = (features.astype(F32) * factor_one).astype(BF16)
    core = lax.psum(t_mm(scaled, grad_one).astype(BF16), ("dp", "ts"))
    return (output.reshape(frames, height, columns, width), t_mm(embed_rows, core))


def solution(mesh):
    placed = (
        P(("dp", "ts"), None, None, None),
        P(),
        P(),
        P(),
        P(),
        P(("dp", "ts"), None),
        P(("dp", "ts"), None),
        P(),
        P(),
        P(("dp", "ts"), None, None, None),
    )
    return jax.shard_map(
        shards,
        mesh=mesh,
        in_specs=placed,
        out_specs=(P(("dp", "ts"), None, None, None), P(("dp", "ts"), None)),
        check_vma=False,
    )
```

profile of v0, /device:TPU:8, one launch (start us, length us, event | category | flops | bytes accessed | tf_op | source)
XLA Modules:
  0.0 330.4 jit_solution(1640951019662262618)
XLA Ops:
  7.2 2.2 collective-permute-start
  9.4 2.5 constant_dynamic-update-slice_fusion.3
  11.9 2.5 constant_dynamic-update-slice_fusion.2
  14.4 1.0 dynamic-slice_convert_fusion
  15.4 0.8 dynamic_slice.10
  16.3 0.8 dynamic_slice.11
  17.0 1.2 convolution_convert_fusion.1
  18.2 1.1 convolution_convert_fusion.3
  20.1 3.5 %fusion.148 = f32[256,256]{1,0:T(8,128)S(1)} fusion(bf16[256,5120]{1,0:T(8,128)(2,1)} %constant_dynamic-update-slice_fusion.2), kind=kOutput, calls=%fused_computation.247 | convolution fusion | flops 671088640 | bytes 2883584 | tf_op jit(solution)/shard_map/dot_general | solution.py:14
  23.7 1.0 convolution_convert_fusion.4
  25.1 0.8 copy-done.8
  30.7 120.0 %all-reduce.4.cloned.1.call-done = bf16[384,384]{1,0:T(8,128)(2,1)} async-done(((bf16[384,384]{1,0:T(8,128)(2,1)}), bf16[384,384]{1,0:T(8,128)(2,1)}) %all-reduce.4.cloned.1.call-update) | async-done | bytes 294928 | tf_op jit(solution)/shard_map/psum | solution.py:96
  150.8 1.1 fusion.7
  153.5 0.9 multiply_reduce_fusion.3
  155.4 1.0 copy.12
  156.5 4.2 %all-to-all-start = ((bf16[2,160,512]{2,0,1:T(2,128)(2,1)}), bf16[2,160,512]{2,0,1:T(2,128)(2,1)}, u32[]{:S(2)}, u32[]{:S(2)}) async-start(bf16[2,160,512]{2,0,1:T(2,128)(2,1)} %copy.12), calls=%async_computation | async-start | bytes 655360 | tf_op jit(solution)/shard_map/all_to_all | solution.py:118
  160.7 6.2 %all-to-all-done = bf16[2,160,512]{2,0,1:T(2,128)(2,1)} async-done(((bf16[2,160,512]{2,0,1:T(2,128)(2,1)}), bf16[2,160,512]{2,0,1:T(2,128)(2,1)}, u32[]{:S(2)}, u32[]{:S(2)}) %all-to-all-start) | async-done | bytes 327712 | tf_op jit(solution)/shard_map/all_to_all | solution.py:118
  166.9 1.8 copy.13
  168.7 1.8 reshape.248
  170.5 1.2 fusion.147
  171.8 1.2 convolution_convert_fusion.7
  174.9 1.8 reshape.249
  176.7 10.8 %all_to_all.30 = bf16[16,20,512]{2,1,0:T(8,128)(2,1)S(1)} all-to-all(bf16[16,20,512]{2,1,0:T(8,128)(2,1)} %reshape.249), channel_id=1, replica_groups={{0,1,2,3,4,5,6,7},{8,9,10,11,12,13,14,15},{16,17,18,19,20,21,22,23},{24..., dimensions={0} | all-to-all | bytes 655360 | tf_op jit(solution)/shard_map/all_to_all | solution.py:127
  187.8 0.9 copy.15
  188.7 1.8 reshape.250
  190.5 1.2 multiply_reduce_fusion.1
  191.7 1.3 convolution_multiply_fusion.6
  193.0 2.4 fusion.16
  196.6 1.0 convolution_convert_fusion.2
  197.7 5.7 %convolution_convert_fusion = bf16[320,5120]{1,0:T(8,128)(2,1)} fusion(bf16[128,5120]{1,0:T(8,128)(2,1)} %param.18, bf16[128,5120]{1,0:T(8,128)(2,1)} %param.17, bf16[128,5120]{1,0:T(8,128)(2,1)} %param.12, bf16[320,128]{1,0:T(8,128)(2,1)S(1)} %slice-done, bf16[320,128]{1,0:T(8,128)(2,1)S(1)} %convolution_convert_fusion.8, bf16[320,128]{1,0:T(8,128)(2,1)S(1)} %fusion.43), kind=kOutput, calls=%fused_computation | convolution fusion | flops 1272463360 | bytes 7454720 | tf_op jit(solution)/shard_map/dot_general | solution.py:14
  203.3 118.4 %all-reduce.6.cloned.1.call-done = bf16[128,384]{1,0:T(8,128)(2,1)} async-done(((bf16[128,384]{1,0:T(8,128)(2,1)}), bf16[128,384]{1,0:T(8,128)(2,1)}) %all-reduce.6.cloned.1.call-update) | async-done | bytes 98320 | tf_op jit(solution)/shard_map/psum | solution.py:143
  321.7 1.9 fusion.129
  (94 shorter events, 11.9 us)
Async XLA Ops:
  7.2 16.5 %copy-start = (bf16[2,4,40,5120]{3,2,1,0:T(8,128)(2,1)S(1)}, bf16[2,4,40,5120]{3,2,1,0:T(8,128)(2,1)}, u32[]{:S(2)}) copy-start(bf16[2,4,40,5120]{3,2,1,0:T(8,128)(2,1)} %param.19) | copy-start | bytes 9830404
  7.2 143.6 %all-reduce.4.cloned.1.call-start = ((), (), s32[]{:S(2)}) async-start(), calls=%async_computation.2 | async-start | bytes 589824 | tf_op jit(solution)/shard_map/psum | solution.py:96
  7.2 17.5 %collective-permute-start = (bf16[2,4,40,128]{3,2,1,0:T(8,128)(2,1)}, bf16[2,4,40,128]{3,2,1,0:T(8,128)(2,1)S(1)}, u32[]{:S(2)}, u32[]{:S(2)}) collective-permute-start(bf16[2,4,40,128]{3,2,1,0:T(8,128)(2,1)} %param.10), channel_id=1, source_target_pairs={{0,1},{1,2},{2,3},{3,4},{4,5},{5,6},{6,7},{7,8},{8,9},{9,10},{10,1... | collective-permute-start | bytes 245768 | tf_op jit(solution)/shard_map/ppermute | solution.py:86
  9.4 7.6 %copy-start.13 = (bf16[160,384]{1,0:T(8,128)(2,1)S(1)}, bf16[160,384]{1,0:T(8,128)(2,1)}, u32[]{:S(2)}) copy-start(bf16[160,384]{1,0:T(8,128)(2,1)} %param.16) | copy-start | bytes 368644
  15.4 2.8 copy-start.6
  20.1 3.6 %copy-start.5 = (bf16[128,5120]{1,0:T(8,128)(2,1)S(1)}, bf16[128,5120]{1,0:T(8,128)(2,1)}, u32[]{:S(2)}) copy-start(bf16[128,5120]{1,0:T(8,128)(2,1)} %param.18) | copy-start | bytes 3932164
  23.6 6.8 %copy-start.3 = (f32[256,256]{1,0:T(8,128)}, f32[256,256]{1,0:T(8,128)S(1)}, u32[]{:S(2)}) copy-start(f32[256,256]{1,0:T(8,128)S(1)} %fusion.148) | copy-start | bytes 786436
  23.7 1.1 copy-start.12
  24.7 1.2 copy-start.8
  150.7 2.5 copy-start.4
  151.9 1.3 copy-start.10
  151.9 2.5 copy-start.14
  152.2 0.8 copy-start.1
  154.7 0.7 copy-start.7
  156.5 10.4 %all-to-all-start = ((bf16[2,160,512]{2,0,1:T(2,128)(2,1)}), bf16[2,160,512]{2,0,1:T(2,128)(2,1)}, u32[]{:S(2)}, u32[]{:S(2)}) async-start(bf16[2,160,512]{2,0,1:T(2,128)(2,1)} %copy.12), calls=%async_computation | async-start | bytes 655360 | tf_op jit(solution)/shard_map/all_to_all | solution.py:118
  160.7 161.0 %all-reduce.6.cloned.1.call-start = ((), (), s32[]{:S(2)}) async-start(), calls=%async_computation.3 | async-start | bytes 196608 | tf_op jit(solution)/shard_map/psum | solution.py:143
  170.5 2.5 copy-start.9
  193.0 2.4 copy-start.2
  193.0 2.4 copy-start.11
  195.7 1.9 slice-start
Sparse Core Ops, SparseCore 0:
  20.2 130.4 all-reduce.3
  197.8 123.8 all-reduce.5
where the time goes:
time: 331 us; the launch traced here: 330 us
  waiting for transfers between devices  245 us (74%)
  matrix products  31.3 us (9%)
  local copies, waits for them, and re-layouts  18.4 us (6%)
  between operations  14.5 us (4%)
  blocking collectives  10.8 us (3%)
  starting transfers between devices  6.42 us (2%)
  other arithmetic  4.29 us (1%)
    psum x1, waiting for transfers between devices, shards(): mixed = lax.psum(part.astype(BF16), ('dp', 'ts'))  120 us
    psum x1, waiting for transfers between devices, shards(): core = lax.psum(t_mm(scaled, grad_one).astype(BF16), ('dp', 'ts'))  118 us
    dot_general x54, matrix products, mm(): return lax.dot_general(a, b, (dims, ((), ())), preferred_element_type=F32)  31.3 us
    all_to_all x1, blocking collectives, shards(): lax.all_to_all(back, 'ts', split_axis=0, concat_axis=1, tiled=True, axis_...  10.8 us
  transfers between devices with their start and end apart: 4, of which 3 were waited for; matrix products, arithmetic and copies ran while one was open for 8% of the time, Pallas kernels for 0%

commit v1 on v0

--- a/solution.py
+++ b/solution.py
@@ -93,7 +93,8 @@
     part = jnp.concatenate(
         [mm(embed_rows, input_spatial), mm((window * gain_t).astype(BF16), input_temporal)], axis=0
     )
-    mixed = lax.psum(part.astype(BF16), ("dp", "ts"))
+    partial = lax.psum(part.astype(BF16), "dp")
+    mixed = lax.psum(partial, "ts")
     map_space, map_time = (mixed[:channels], mixed[channels:])
     gram = mm_t(basis, basis)
     cotangent_rows = cotangent.reshape(tokens, width)

time: 331 us -> 320 us (0.967)
  waiting for transfers between devices: 245 us -> 234 us
    psum x1 -> x2, waiting for transfers between devices: 120 us -> 109 us  [the longest x1 94.4 us: shards(): mixed = lax.psum(partial, 'ts')]
  transfers between devices with their start and end apart: 4 -> 5, of which waited for: 3 -> 4; matrix products, arithmetic and copies ran while one was open for 8% -> 8% of each run, Pallas kernels for 0% -> 0%
where the time goes in v1:
time: 320 us; the launch traced here: 319 us
  waiting for transfers between devices  234 us (73%)
  matrix products  31.3 us (10%)
  local copies, waits for them, and re-layouts  18.4 us (6%)
  between operations  14.2 us (4%)
  blocking collectives  10.8 us (3%)
  starting transfers between devices  6.81 us (2%)
  other arithmetic  4.3 us (1%)
    psum x1, waiting for transfers between devices, shards(): core = lax.psum(t_mm(scaled, grad_one).astype(BF16), ('dp', 'ts'))  118 us
    psum x1, waiting for transfers between devices, shards(): mixed = lax.psum(partial, 'ts')  94.4 us
    dot_general x54, matrix products, mm(): return lax.dot_general(a, b, (dims, ((), ())), preferred_element_type=F32)  31.3 us
    psum x1, waiting for transfers between devices, shards(): partial = lax.psum(part.astype(BF16), 'dp')  14.8 us
    all_to_all x1, blocking collectives, shards(): lax.all_to_all(back, 'ts', split_axis=0, concat_axis=1, tiled=True, axis_...  10.8 us
  transfers between devices with their start and end apart: 5, of which 4 were waited for; matrix products, arithmetic and copies ran while one was open for 8% of the time, Pallas kernels for 0%

profile of v1, /device:TPU:8, one launch (start us, length us, event | category | flops | bytes accessed | tf_op | source)
XLA Modules:
  0.0 319.5 jit_solution(12852479243256317759)
XLA Ops:
  7.2 2.2 collective-permute-start
  9.4 2.5 constant_dynamic-update-slice_fusion.3
  11.9 2.5 constant_dynamic-update-slice_fusion.2
  14.4 1.0 dynamic-slice_convert_fusion
  15.4 0.8 dynamic_slice.10
  17.0 1.2 convolution_convert_fusion.1
  18.2 1.1 convolution_convert_fusion.3
  20.2 3.5 %fusion.148 = f32[256,256]{1,0:T(8,128)S(1)} fusion(bf16[256,5120]{1,0:T(8,128)(2,1)} %constant_dynamic-update-slice_fusion.2), kind=kOutput, calls=%fused_computation.247 | convolution fusion | flops 671088640 | bytes 2883584 | tf_op jit(solution)/shard_map/dot_general | solution.py:14
  23.7 1.0 convolution_convert_fusion.4
  25.1 0.8 copy-done.8
  30.8 14.8 %all-reduce.5.cloned.1.call-done = bf16[384,384]{1,0:T(8,128)(2,1)} async-done(((bf16[384,384]{1,0:T(8,128)(2,1)}), bf16[384,384]{1,0:T(8,128)(2,1)}) %all-reduce.5.cloned.1.call-update) | async-done | bytes 294928 | tf_op jit(solution)/shard_map/psum | solution.py:96
  45.6 94.4 %all-reduce.7.cloned.1.call-done = bf16[384,384]{1,0:T(8,128)(2,1)} async-done(((bf16[384,384]{1,0:T(8,128)(2,1)}), bf16[384,384]{1,0:T(8,128)(2,1)}) %all-reduce.7.cloned.1.call-update) | async-done | bytes 294928 | tf_op jit(solution)/shard_map/psum | solution.py:97
  140.1 1.1 fusion.7
  142.8 0.9 multiply_reduce_fusion.3
  144.7 1.0 copy.12
  145.8 4.5 %all-to-all-start = ((bf16[2,160,512]{2,0,1:T(2,128)(2,1)}), bf16[2,160,512]{2,0,1:T(2,128)(2,1)}, u32[]{:S(2)}, u32[]{:S(2)}) async-start(bf16[2,160,512]{2,0,1:T(2,128)(2,1)} %copy.12), calls=%async_computation | async-start | bytes 655360 | tf_op jit(solution)/shard_map/all_to_all | solution.py:119
  150.3 6.3 %all-to-all-done = bf16[2,160,512]{2,0,1:T(2,128)(2,1)} async-done(((bf16[2,160,512]{2,0,1:T(2,128)(2,1)}), bf16[2,160,512]{2,0,1:T(2,128)(2,1)}, u32[]{:S(2)}, u32[]{:S(2)}) %all-to-all-start) | async-done | bytes 327712 | tf_op jit(solution)/shard_map/all_to_all | solution.py:119
  156.6 1.8 copy.13
  158.3 1.8 reshape.248
  160.1 1.2 fusion.147
  161.5 1.2 convolution_convert_fusion.7
  164.6 1.8 reshape.249
  166.3 10.8 %all_to_all.30 = bf16[16,20,512]{2,1,0:T(8,128)(2,1)S(1)} all-to-all(bf16[16,20,512]{2,1,0:T(8,128)(2,1)} %reshape.249), channel_id=1, replica_groups={{0,1,2,3,4,5,6,7},{8,9,10,11,12,13,14,15},{16,17,18,19,20,21,22,23},{24..., dimensions={0} | all-to-all | bytes 655360 | tf_op jit(solution)/shard_map/all_to_all | solution.py:128
  177.5 0.9 copy.15
  178.4 1.8 reshape.250
  180.2 1.2 multiply_reduce_fusion.1
  181.4 1.3 convolution_multiply_fusion.6
  182.7 2.4 fusion.16
  186.3 1.0 convolution_convert_fusion.2
  187.3 5.7 %convolution_convert_fusion = bf16[320,5120]{1,0:T(8,128)(2,1)} fusion(bf16[128,5120]{1,0:T(8,128)(2,1)} %param.18, bf16[128,5120]{1,0:T(8,128)(2,1)} %param.17, bf16[128,5120]{1,0:T(8,128)(2,1)} %param.12, bf16[320,128]{1,0:T(8,128)(2,1)S(1)} %slice-done, bf16[320,128]{1,0:T(8,128)(2,1)S(1)} %convolution_convert_fusion.8, bf16[320,128]{1,0:T(8,128)(2,1)S(1)} %fusion.43), kind=kOutput, calls=%fused_computation | convolution fusion | flops 1272463360 | bytes 7454720 | tf_op jit(solution)/shard_map/dot_general | solution.py:14
  193.0 118.1 %all-reduce.9.cloned.1.call-done = bf16[128,384]{1,0:T(8,128)(2,1)} async-done(((bf16[128,384]{1,0:T(8,128)(2,1)}), bf16[128,384]{1,0:T(8,128)(2,1)}) %all-reduce.9.cloned.1.call-update) | async-done | bytes 98320 | tf_op jit(solution)/shard_map/psum | solution.py:144
  311.1 1.9 fusion.129
  (97 shorter events, 12.8 us)
Async XLA Ops:
  7.2 16.5 %copy-start = (bf16[2,4,40,5120]{3,2,1,0:T(8,128)(2,1)S(1)}, bf16[2,4,40,5120]{3,2,1,0:T(8,128)(2,1)}, u32[]{:S(2)}) copy-start(bf16[2,4,40,5120]{3,2,1,0:T(8,128)(2,1)} %param.19) | copy-start | bytes 9830404
  7.2 38.4 %all-reduce.5.cloned.1.call-start = ((), (), s32[]{:S(2)}) async-start(), calls=%async_computation.2 | async-start | bytes 589824 | tf_op jit(solution)/shard_map/psum | solution.py:96
  7.2 17.5 %collective-permute-start = (bf16[2,4,40,128]{3,2,1,0:T(8,128)(2,1)}, bf16[2,4,40,128]{3,2,1,0:T(8,128)(2,1)S(1)}, u32[]{:S(2)}, u32[]{:S(2)}) collective-permute-start(bf16[2,4,40,128]{3,2,1,0:T(8,128)(2,1)} %param.10), channel_id=1, source_target_pairs={{0,1},{1,2},{2,3},{3,4},{4,5},{5,6},{6,7},{7,8},{8,9},{9,10},{10,1... | collective-permute-start | bytes 245768 | tf_op jit(solution)/shard_map/ppermute | solution.py:86
  9.4 7.6 %copy-start.13 = (bf16[160,384]{1,0:T(8,128)(2,1)S(1)}, bf16[160,384]{1,0:T(8,128)(2,1)}, u32[]{:S(2)}) copy-start(bf16[160,384]{1,0:T(8,128)(2,1)} %param.16) | copy-start | bytes 368644
  15.4 2.8 copy-start.6
  20.1 120.0 %all-reduce.7.cloned.1.call-start = ((), (), s32[]{:S(2)}) async-start(), calls=%async_computation.3 | async-start | bytes 589824 | tf_op jit(solution)/shard_map/psum | solution.py:97
  20.1 3.5 %copy-start.5 = (bf16[128,5120]{1,0:T(8,128)(2,1)S(1)}, bf16[128,5120]{1,0:T(8,128)(2,1)}, u32[]{:S(2)}) copy-start(bf16[128,5120]{1,0:T(8,128)(2,1)} %param.18) | copy-start | bytes 3932164
  23.7 6.8 %copy-start.3 = (f32[256,256]{1,0:T(8,128)}, f32[256,256]{1,0:T(8,128)S(1)}, u32[]{:S(2)}) copy-start(f32[256,256]{1,0:T(8,128)S(1)} %fusion.148) | copy-start | bytes 786436
  23.7 1.1 copy-start.12
  24.7 1.2 copy-start.8
  140.1 2.5 copy-start.4
  141.2 1.3 copy-start.10
  141.2 2.5 copy-start.14
  141.5 0.8 copy-start.1
  144.0 0.7 copy-start.7
  145.8 10.8 %all-to-all-start = ((bf16[2,160,512]{2,0,1:T(2,128)(2,1)}), bf16[2,160,512]{2,0,1:T(2,128)(2,1)}, u32[]{:S(2)}, u32[]{:S(2)}) async-start(bf16[2,160,512]{2,0,1:T(2,128)(2,1)} %copy.12), calls=%async_computation | async-start | bytes 655360 | tf_op jit(solution)/shard_map/all_to_all | solution.py:119
  150.3 160.8 %all-reduce.9.cloned.1.call-start = ((), (), s32[]{:S(2)}) async-start(), calls=%async_computation.4 | async-start | bytes 196608 | tf_op jit(solution)/shard_map/psum | solution.py:144
  160.1 2.5 copy-start.9
  182.7 2.4 copy-start.2
  182.7 2.4 copy-start.11
  185.4 1.9 slice-start
Sparse Core Ops, SparseCore 0:
  20.2 25.3 all-reduce.4
  49.0 91.0 all-reduce.6
  187.4 123.6 all-reduce.8
